TPU v7x, 32 devices: a whole 2x2x4 slice. The times are simulated.
32 devices in a mesh: groups: 2 (over y), ctx: 4 (over z), chan: 4 (over x, core).
Axes of the slice: x: 2, y: 2, z: 4, core: 2. Of those that a mesh axis runs over, the one named last changes fastest.
Arguments:
- query_gate: float32 [4096, 1024], P(('groups', 'ctx'), 'chan'), parts along dimension 0, may hold values from -6 to 6
- key_gate: float32 [4096, 1024], P(('groups', 'ctx'), 'chan'), parts along dimension 0, may hold values from -6 to 6
- values: float32 [4096, 1024], P(('groups', 'ctx'), 'chan'), parts along dimension 0, may hold values from -6 to 6
- filter_taps: float32 [4096, 1024], P(None, 'chan'), may hold values from -0.125 to 0.125
- skip_gain: float32 [1024], P('chan'), may hold values from -1 to 1
- upstream: float32 [4096, 1024], P(('groups', 'ctx'), 'chan'), parts along dimension 0, may hold values from -6 to 6
Outputs:
- query_grad: float32 [4096, 1024], P(('groups', 'ctx'), 'chan'), parts along dimension 0
- key_grad: float32 [4096, 1024], P(('groups', 'ctx'), 'chan'), parts along dimension 0
- value_grad: float32 [4096, 1024], P(('groups', 'ctx'), 'chan'), parts along dimension 0
- filter_grad: float32 [8192, 1024], P(('groups', 'ctx'), 'chan'), parts along dimension 0
- skip_grad: float32 [2048], P(('groups', 'chan')), parts along dimension 0
There are 2 independent parts, one for each index of `groups`. A program takes and returns all parts, laid end to end along the dimension named above; an argument that names none is the same for every part. Nothing has to cross between parts.
All inputs are finite; a program needn't handle non-finite values.
Results may differ from a plain program's by a relative error of at most 0.0001.
Values sent between devices are 32-bit elements; how exact they have to be, the bound alone decides.
No kernel may reach another device: no remote copies, remote signals or barrier semaphores. Data moves between devices by JAX's collectives and lax.ppermute only.
A program may use at most 128 MiB of HBM per device.

v0:
```python
import math
import jax
import jax.numpy as jnp
from jax import lax
from jax.sharding import PartitionSpec as P


def matmul(left, right):
    return jnp.dot(left, right, preferred_element_type=jnp.float32, precision=lax.Precision.HIGHEST)


def forward_table(seg_len, count, offset):
    num_bins = seg_len + 1
    period = 2 * seg_len
    bin_index = lax.broadcasted_iota(jnp.int32, (num_bins, count), 0)
    pos_index = lax.broadcasted_iota(jnp.int32, (num_bins, count), 1) + offset
    angles = (bin_index * pos_index % period).astype(jnp.float32) * (2.0 * math.pi / period)
    return jnp.concatenate([jnp.cos(angles), -jnp.sin(angles)], axis=0)


def inverse_table(seg_len, count, offset):
    num_bins = seg_len + 1
    period = 2 * seg_len
    pos_index = lax.broadcasted_iota(jnp.int32, (count, num_bins), 0) + offset
    bin_index = lax.broadcasted_iota(jnp.int32, (count, num_bins), 1)
    angles = (bin_index * pos_index % period).astype(jnp.float32) * (2.0 * math.pi / period)
    weights = jnp.where((bin_index == 0) | (bin_index == seg_len), 1.0, 2.0) / period
    return jnp.concatenate([weights * jnp.cos(angles), -weights * jnp.sin(angles)], axis=1)


def times_spec(first, second):
    num_bins = first.shape[0] // 2
    real_a, imag_a = (first[:num_bins], first[num_bins:])
    real_b, imag_b = (second[:num_bins], second[num_bins:])
    return jnp.concatenate(
        [real_a * real_b - imag_a * imag_b, real_a * imag_b + imag_a * real_b], axis=0
    )


def conj_times(first, second):
    num_bins = first.shape[0] // 2
    real_a, imag_a = (first[:num_bins], first[num_bins:])
    real_b, imag_b = (second[:num_bins], second[num_bins:])
    return jnp.concatenate(
        [real_a * real_b + imag_a * imag_b, real_a * imag_b - imag_a * real_b], axis=0
    )


def pick(stack, index):
    return lax.dynamic_index_in_dim(stack, index, 0, keepdims=False)


def local(query_gate, key_gate, values, filter_taps, skip_gain, upstream):
    seg_len, width_dev = values.shape
    cycle_size = lax.axis_size("ctx")
    position = lax.axis_index("ctx")
    history = seg_len * cycle_size
    gated = key_gate * values
    mixed_grad = upstream * query_gate
    table_low = forward_table(seg_len, seg_len, 0)
    table_high = forward_table(seg_len, seg_len, seg_len)
    table_taps = forward_table(seg_len, 2 * seg_len, 0)
    back_low = inverse_table(seg_len, seg_len, 0)
    back_high = inverse_table(seg_len, seg_len, seg_len)
    back_full = inverse_table(seg_len, 2 * seg_len, 0)
    own_grad_spec = matmul(table_high, mixed_grad)
    spec_rows = 2 * (seg_len + 1)

    def taps_spec(lag_block):
        start_row = (lag_block - 1) * seg_len + history
        window = lax.dynamic_slice_in_dim(filter_taps, start_row, 2 * seg_len, 0)
        return matmul(table_taps, window)

    def visit(carry, gated_spec, grad_spec, source):
        acc_conv, acc_back, partial_value = carry
        lag_block = position - source
        acc_conv = acc_conv + times_spec(taps_spec(lag_block), gated_spec)
        acc_back = acc_back + conj_times(taps_spec(-lag_block), grad_spec)
        segment = matmul(back_full, conj_times(gated_spec, own_grad_spec))
        start_row = (lag_block - 1) * seg_len + history
        current = lax.dynamic_slice_in_dim(partial_value, start_row, 2 * seg_len, 0)
        partial_value = lax.dynamic_update_slice_in_dim(
            partial_value, current + segment, start_row, 0
        )
        return (acc_conv, acc_back, partial_value)

    initial = (
        jnp.zeros((spec_rows, width_dev), jnp.float32),
        jnp.zeros((spec_rows, width_dev), jnp.float32),
        jnp.zeros((2 * history, width_dev), jnp.float32),
    )
    own_gated_spec = matmul(table_low, gated)
    pieces = (
        lax.all_gather(own_gated_spec[None], "ctx", axis=0, tiled=True),
        lax.all_gather(own_grad_spec[None], "ctx", axis=0, tiled=True),
    )

    def advance(member, state):
        return visit(state, pick(pieces[0], member), pick(pieces[1], member), member)

    folded = lax.fori_loop(0, pieces[0].shape[0], advance, initial)
    acc_conv, acc_back, partial_value = folded
    filter_grad = lax.psum_scatter(partial_value, "ctx", scatter_dimension=0, tiled=True)
    conv = matmul(back_high, acc_conv)
    back = matmul(back_low, acc_back) + skip_gain[None, :] * mixed_grad
    query_grad = upstream * (conv + skip_gain[None, :] * gated)
    key_grad = back * values
    value_grad = back * key_gate
    skip_grad = lax.psum(jnp.sum(mixed_grad * gated, axis=0), "ctx")
    return (query_grad, key_grad, value_grad, filter_grad, skip_grad)


def solution(mesh):
    in_specs = (
        P(("groups", "ctx"), "chan"),
        P(("groups", "ctx"), "chan"),
        P(("groups", "ctx"), "chan"),
        P(None, "chan"),
        P("chan"),
        P(("groups", "ctx"), "chan"),
    )
    out_specs = (
        P(("groups", "ctx"), "chan"),
        P(("groups", "ctx"), "chan"),
        P(("groups", "ctx"), "chan"),
        P(("groups", "ctx"), "chan"),
        P(("groups", "chan")),
    )
    return jax.shard_map(local, mesh=mesh, in_specs=in_specs, out_specs=out_specs, check_vma=False)
```

profile of v0, /device:TPU:0, one launch (start us, length us, event | category | flops | bytes accessed | tf_op | source)
XLA Modules:
  0.0 386.1 jit_solution(120343839279487304)
XLA Ops:
  7.2 4.2 %sine_negate_fusion.2 = (f32[513,512]{1,0:T(8,128)S(1)}, f32[513,512]{1,0:T(8,128)S(1)}) fusion(), kind=kLoop, calls=%fused_computation.105 | loop fusion | flops 3939840 | bytes 2101248 | tf_op jit(solution)/shard_map/neg | solution.py:18
  11.4 2.9 convolution_bitcast_fusion.3
  14.4 0.6 all-gather.9.cloned.1.call-start
  14.9 4.2 %fusion.71 = (f32[513,512]{1,0:T(8,128)S(1)}, f32[513,512]{1,0:T(8,128)S(1)}) fusion(s32[512]{0:T(512)S(1)} %iota_add_fusion), kind=kLoop, calls=%fused_computation.112 | loop fusion | flops 3939840 | bytes 2103296 | tf_op jit(solution)/shard_map/cos | solution.py:18
  19.1 2.8 fusion.32
  22.0 1.4 reduce-scatter.2.cloned.1.call-start
  23.5 8.4 %sine_negate_fusion = (f32[513,1024]{1,0:T(8,128)S(1)}, f32[513,1024]{1,0:T(8,128)S(1)}) fusion(), kind=kLoop, calls=%fused_computation.54 | loop fusion | flops 7879680 | bytes 4202496 | tf_op jit(solution)/shard_map/neg | solution.py:18
  31.8 10.6 %sine_multiply_fusion = (f32[1024,513]{1,0:T(8,128)S(1)}, f32[1024,513]{1,0:T(8,128)S(1)}) fusion(f32[513]{0:T(1024)S(1)} %fusion.73, f32[513]{0:T(1024)S(1)} %select_multiply_fusion), kind=kLoop, calls=%fused_computation.38 | loop fusion | flops 8404992 | bytes 4206600 | tf_op jit(solution)/shard_map/mul | solution.py:28
  42.4 2.5 pad_maximum_fusion.1
  44.9 2.9 pad_maximum_fusion
  47.9 50.6 %all-gather.7.cloned.1.call-done = f32[4,1026,256]{2,1,0:T(8,128)} async-done(((f32[1,1026,256]{2,1,0:T(8,128)}), f32[4,1026,256]{2,1,0:T(8,128)}) %all-gather.7.cloned.1.call-update) | async-done | bytes 4202512 | tf_op jit(solution)/shard_map/all_gather | solution.py:94
  98.5 81.4 %all-gather.9.cloned.1.call-done = f32[4,1026,256]{2,1,0:T(8,128)} async-done(((f32[1,1026,256]{2,1,0:T(8,128)}), f32[4,1026,256]{2,1,0:T(8,128)}) %all-gather.9.cloned.1.call-update) | async-done | bytes 4202512 | tf_op jit(solution)/shard_map/all_gather | solution.py:95
  179.9 2.3 broadcast_in_dim.27.clone
  182.2 121.5 %while.21 = (s32[]{:T(128)}, f32[1026,256]{1,0:T(8,128)}, f32[1026,256]{1,0:T(8,128)}, f32[4096,256]{1,0:T(8,128)}, s32[]{:T(128)}, /*index=5*/f32[4096,256]{1,0...) while((s32[]{:T(128)}, f32[1026,256]{1,0:T(8,128)}, ...), condition=%wide.region_1.2_spmd.clone, body=%wide.region_0.1_spmd.clone.sunk | while | flops 9687015424 | bytes 64113172 | solution.py:101
  182.6 5.7 %convolution_bitcast_fusion.6 = f32[1026,256]{1,0:T(8,128)S(1)} fusion(f32[1026,1024]{1,0:T(8,128)} %get-tuple-element.519, f32[4096,256]{1,0:T(8,128)} %get-tuple-element.518, s32[]{:T(128)S(6)} %select_n.167), kind=kOutput, calls=%fused_computation.1.clone.1 | convolution fusion | flops 3227516928 | bytes 6326276 | tf_op jit(solution)/shard_map/while/body/eval_jaxpr/dot_general | solution.py:9
  188.3 1.6 multiply_add_fusion.5
  189.9 5.7 %convolution_bitcast_fusion.7 = f32[1026,256]{1,0:T(8,128)S(1)} fusion(f32[1026,1024]{1,0:T(8,128)} %get-tuple-element.519, f32[4096,256]{1,0:T(8,128)} %get-tuple-element.518, s32[]{:T(128)S(6)} %select_n.168), kind=kOutput, calls=%fused_computation.clone.1 | convolution fusion | flops 3227516928 | bytes 6326276 | tf_op jit(solution)/shard_map/while/body/eval_jaxpr/dot_general | solution.py:9
  195.6 1.6 multiply_add_fusion.6
  197.5 0.6 maximum_add_fusion.3
  198.1 1.0 copy-done.3
  199.1 0.3 copy-done.6
  199.4 1.3 constant_dynamic-slice_fusion.2
  200.7 0.3 copy.19
  201.1 9.8 %fusion.98 = f32[1024,256]{0,1:T(8,128)S(1)} fusion(f32[1024,256]{0,1:T(8,128)S(1)} %copy.19, f32[1024,1026]{1,0:T(8,128)} %get-tuple-element.523, f32[513,256]{1,0:T(8,128)S(1)} %get-tuple-element.475, f32[513,256]{1,0:T(8,128)S(1)} %get-tuple-element.476), kind=kOutput, calls=%fused_computation.3.clone.1 | convolution fusion | flops 3228041728 | bytes 7350272 | tf_op jit(solution)/shard_map/while/body/eval_jaxpr/dot_general | solution.py:9
  211.3 1.1 constant_dynamic-update-slice_fusion.2
  212.3 0.5 copy-done.1
  212.9 5.7 %convolution_bitcast_fusion.6 = f32[1026,256]{1,0:T(8,128)S(1)} fusion(f32[1026,1024]{1,0:T(8,128)} %get-tuple-element.519, f32[4096,256]{1,0:T(8,128)} %get-tuple-element.518, s32[]{:T(128)S(6)} %select_n.167), kind=kOutput, calls=%fused_computation.1.clone.1 | convolution fusion | flops 3227516928 | bytes 6326276 | tf_op jit(solution)/shard_map/while/body/eval_jaxpr/dot_general | solution.py:9
  218.6 1.6 multiply_add_fusion.5
  220.2 5.7 %convolution_bitcast_fusion.7 = f32[1026,256]{1,0:T(8,128)S(1)} fusion(f32[1026,1024]{1,0:T(8,128)} %get-tuple-element.519, f32[4096,256]{1,0:T(8,128)} %get-tuple-element.518, s32[]{:T(128)S(6)} %select_n.168), kind=kOutput, calls=%fused_computation.clone.1 | convolution fusion | flops 3227516928 | bytes 6326276 | tf_op jit(solution)/shard_map/while/body/eval_jaxpr/dot_general | solution.py:9
  225.9 1.6 multiply_add_fusion.6
  227.7 0.6 maximum_add_fusion.3
  228.4 1.0 copy-done.3
  229.4 0.3 copy-done.6
  229.7 1.3 constant_dynamic-slice_fusion.2
  231.3 9.8 %fusion.98 = f32[1024,256]{0,1:T(8,128)S(1)} fusion(f32[1024,256]{0,1:T(8,128)S(1)} %copy.19, f32[1024,1026]{1,0:T(8,128)} %get-tuple-element.523, f32[513,256]{1,0:T(8,128)S(1)} %get-tuple-element.475, f32[513,256]{1,0:T(8,128)S(1)} %get-tuple-element.476), kind=kOutput, calls=%fused_computation.3.clone.1 | convolution fusion | flops 3228041728 | bytes 7350272 | tf_op jit(solution)/shard_map/while/body/eval_jaxpr/dot_general | solution.py:9
  241.5 1.1 constant_dynamic-update-slice_fusion.2
  242.6 0.5 copy-done.1
  243.1 5.7 %convolution_bitcast_fusion.6 = f32[1026,256]{1,0:T(8,128)S(1)} fusion(f32[1026,1024]{1,0:T(8,128)} %get-tuple-element.519, f32[4096,256]{1,0:T(8,128)} %get-tuple-element.518, s32[]{:T(128)S(6)} %select_n.167), kind=kOutput, calls=%fused_computation.1.clone.1 | convolution fusion | flops 3227516928 | bytes 6326276 | tf_op jit(solution)/shard_map/while/body/eval_jaxpr/dot_general | solution.py:9
  248.8 1.6 multiply_add_fusion.5
  250.4 5.7 %convolution_bitcast_fusion.7 = f32[1026,256]{1,0:T(8,128)S(1)} fusion(f32[1026,1024]{1,0:T(8,128)} %get-tuple-element.519, f32[4096,256]{1,0:T(8,128)} %get-tuple-element.518, s32[]{:T(128)S(6)} %select_n.168), kind=kOutput, calls=%fused_computation.clone.1 | convolution fusion | flops 3227516928 | bytes 6326276 | tf_op jit(solution)/shard_map/while/body/eval_jaxpr/dot_general | solution.py:9
  256.1 1.6 multiply_add_fusion.6
  258.0 0.6 maximum_add_fusion.3
  258.6 1.0 copy-done.3
  259.6 0.3 copy-done.6
  260.0 1.3 constant_dynamic-slice_fusion.2
  261.6 9.8 %fusion.98 = f32[1024,256]{0,1:T(8,128)S(1)} fusion(f32[1024,256]{0,1:T(8,128)S(1)} %copy.19, f32[1024,1026]{1,0:T(8,128)} %get-tuple-element.523, f32[513,256]{1,0:T(8,128)S(1)} %get-tuple-element.475, f32[513,256]{1,0:T(8,128)S(1)} %get-tuple-element.476), kind=kOutput, calls=%fused_computation.3.clone.1 | convolution fusion | flops 3228041728 | bytes 7350272 | tf_op jit(solution)/shard_map/while/body/eval_jaxpr/dot_general | solution.py:9
  271.8 1.0 constant_dynamic-update-slice_fusion.2
  272.8 0.6 copy-done.1
  273.4 5.7 %convolution_bitcast_fusion.6 = f32[1026,256]{1,0:T(8,128)S(1)} fusion(f32[1026,1024]{1,0:T(8,128)} %get-tuple-element.519, f32[4096,256]{1,0:T(8,128)} %get-tuple-element.518, s32[]{:T(128)S(6)} %select_n.167), kind=kOutput, calls=%fused_computation.1.clone.1 | convolution fusion | flops 3227516928 | bytes 6326276 | tf_op jit(solution)/shard_map/while/body/eval_jaxpr/dot_general | solution.py:9
  279.1 1.6 multiply_add_fusion.5
  280.7 5.7 %convolution_bitcast_fusion.7 = f32[1026,256]{1,0:T(8,128)S(1)} fusion(f32[1026,1024]{1,0:T(8,128)} %get-tuple-element.519, f32[4096,256]{1,0:T(8,128)} %get-tuple-element.518, s32[]{:T(128)S(6)} %select_n.168), kind=kOutput, calls=%fused_computation.clone.1 | convolution fusion | flops 3227516928 | bytes 6326276 | tf_op jit(solution)/shard_map/while/body/eval_jaxpr/dot_general | solution.py:9
  286.4 1.6 multiply_add_fusion.6
  288.3 0.6 maximum_add_fusion.3
  288.9 1.0 copy-done.3
  289.9 0.3 copy-done.6
  290.2 1.3 constant_dynamic-slice_fusion.2
  291.9 9.8 %fusion.98 = f32[1024,256]{0,1:T(8,128)S(1)} fusion(f32[1024,256]{0,1:T(8,128)S(1)} %copy.19, f32[1024,1026]{1,0:T(8,128)} %get-tuple-element.523, f32[513,256]{1,0:T(8,128)S(1)} %get-tuple-element.475, f32[513,256]{1,0:T(8,128)S(1)} %get-tuple-element.476), kind=kOutput, calls=%fused_computation.3.clone.1 | convolution fusion | flops 3228041728 | bytes 7350272 | tf_op jit(solution)/shard_map/while/body/eval_jaxpr/dot_general | solution.py:9
  302.0 1.1 constant_dynamic-update-slice_fusion.2
  303.1 0.5 copy-done.1
  303.7 11.6 %sine_multiply_fusion.1 = (f32[512,513]{1,0:T(8,128)S(1)}, f32[512,513]{1,0:T(8,128)S(1)}, f32[512,513]{1,0:T(8,128)}, f32[512,513]{1,0:T(8,128)S(1)}) fusion(f32[513]{0:T(1024)S(1)} %fusion.73, s32[512]{0:T(512)S(1)} %iota_add_fusion, f32[513]{0:T(1024)S(1)} %select_multiply_fusion), kind=kLoop, calls=%fused_computation.83 | loop fusion | flops 8404992 | bytes 4208648 | tf_op jit(solution)/shard_map/mul | solution.py:28
  315.3 3.4 multiply_reduce_fusion
  318.7 9.7 %psum.7 = f32[256]{0:T(256)} all-reduce(f32[256]{0:T(256)S(1)} %get-tuple-element.376), channel_id=1, replica_groups=mesh['groups'=2,'ctx'=4,'chan'=4] {'ctx'}, use_global_device_ids=true, to_apply=%region_4.5 | all-reduce | flops 256 | bytes 2048 | tf_op jit(solution)/shard_map/psum | solution.py:109
  328.4 4.6 %fusion.54 = f32[512,256]{1,0:T(8,128)} fusion(f32[512,256]{1,0:T(8,128)S(1)} %copy-done.9, f32[1026,256]{1,0:T(8,128)S(1)} %copy-done.7, f32[512,513]{1,0:T(8,128)S(1)} %get-tuple-element.382, f32[512,513]{1,0:T(8,128)} %get-tuple-element.390, f32[256]{0:T(256)S(1)} %copy-done.16, f32[512,256]{1,0:T(8,128)S(1)} %copy-done.11, f32[512,256]{1,0:T(8,128)} %param.10), kind=kOutput, calls=%fused_computation.95 | convolution fusion | flops 1614808064 | bytes 5250048 | tf_op jit(solution)/shard_map/dot_general | solution.py:9
  333.1 46.3 %reduce-scatter.2.cloned.1.call-done = f32[1024,256]{1,0:T(8,128)} async-done(((f32[4096,256]{1,0:T(8,128)}), f32[1024,256]{1,0:T(8,128)}) %reduce-scatter.2.cloned.1.call-update) | async-done | bytes 1048592 | tf_op jit(solution)/shard_map/reduce_scatter | solution.py:103
  (68 shorter events, 3.5 us)
Async XLA Ops:
  7.2 4.3 %copy-start.10 = (f32[512,256]{1,0:T(8,128)S(1)}, f32[512,256]{1,0:T(8,128)}, u32[]{:S(2)}) copy-start(f32[512,256]{1,0:T(8,128)} %param.9) | copy-start | bytes 1572868
  7.2 4.3 %copy-start.12 = (f32[512,256]{1,0:T(8,128)S(1)}, f32[512,256]{1,0:T(8,128)}, u32[]{:S(2)}) copy-start(f32[512,256]{1,0:T(8,128)} %param.10) | copy-start | bytes 1572868
  7.2 91.3 %all-gather.7.cloned.1.call-start = ((), (), s32[]{:S(2)}) async-start(), calls=%async_computation.2 | async-start | bytes 5283840 | tf_op jit(solution)/shard_map/all_gather | solution.py:94
  14.3 4.8 %copy-start.8 = (f32[512,256]{1,0:T(8,128)S(1)}, f32[512,256]{1,0:T(8,128)}, u32[]{:S(2)}) copy-start(f32[512,256]{1,0:T(8,128)} %param.13) | copy-start | bytes 1572868
  14.3 4.8 %copy-start.14 = (f32[512,256]{1,0:T(8,128)S(1)}, f32[512,256]{1,0:T(8,128)}, u32[]{:S(2)}) copy-start(f32[512,256]{1,0:T(8,128)} %param.8) | copy-start | bytes 1572868
  14.4 165.6 %all-gather.9.cloned.1.call-start = ((), (), s32[]{:S(2)}) async-start(), calls=%async_computation.3 | async-start | bytes 5283840 | tf_op jit(solution)/shard_map/all_gather | solution.py:95
  22.0 357.4 %reduce-scatter.2.cloned.1.call-start = ((), (), s32[]{:S(2)}) async-start(), calls=%async_computation.1 | async-start | bytes 5242880 | tf_op jit(solution)/shard_map/reduce_scatter | solution.py:103
  47.9 134.3 %copy-start = (f32[1026,256]{1,0:T(8,128)S(1)}, f32[1026,256]{1,0:T(8,128)}, u32[]{:S(2)}) copy-start(f32[1026,256]{1,0:T(8,128)} %fusion.32) | copy-start | bytes 3151876
  195.6 1.6 copy-start.2
  195.6 1.9 copy-start.5
  198.1 1.0 copy-start.3
  198.1 1.3 copy-start.6
  211.3 1.6 copy-start.1
  225.9 1.6 copy-start.2
  225.9 1.9 copy-start.5
  228.4 1.0 copy-start.3
  228.4 1.3 copy-start.6
  241.5 1.6 copy-start.1
  256.1 1.6 copy-start.2
  256.1 1.9 copy-start.5
  258.6 1.0 copy-start.3
  258.6 1.3 copy-start.6
  271.8 1.6 copy-start.1
  286.4 1.6 copy-start.2
  286.4 1.9 copy-start.5
  288.9 1.0 copy-start.3
  288.9 1.3 copy-start.6
  302.0 1.6 copy-start.1
  303.7 11.6 %copy-start.4 = (f32[1026,256]{1,0:T(8,128)S(1)}, f32[1026,256]{1,0:T(8,128)}, u32[]{:S(2)}) copy-start(f32[1026,256]{1,0:T(8,128)} %get-tuple-element.538) | copy-start | bytes 3151876
  303.7 11.6 %copy-start.9 = (f32[512,256]{1,0:T(8,128)S(1)}, f32[512,256]{1,0:T(8,128)}, u32[]{:S(2)}) copy-start(f32[512,256]{1,0:T(8,128)} %param.13) | copy-start | bytes 1572868
  303.7 11.6 %copy-start.11 = (f32[512,256]{1,0:T(8,128)S(1)}, f32[512,256]{1,0:T(8,128)}, u32[]{:S(2)}) copy-start(f32[512,256]{1,0:T(8,128)} %param.9) | copy-start | bytes 1572868
  303.7 11.6 %copy-start.13 = (f32[512,256]{1,0:T(8,128)S(1)}, f32[512,256]{1,0:T(8,128)}, u32[]{:S(2)}) copy-start(f32[512,256]{1,0:T(8,128)} %param.10) | copy-start | bytes 1572868
  303.7 11.6 %copy-start.15 = (f32[512,256]{1,0:T(8,128)S(1)}, f32[512,256]{1,0:T(8,128)}, u32[]{:S(2)}) copy-start(f32[512,256]{1,0:T(8,128)} %param.8) | copy-start | bytes 1572868
  303.7 11.6 %copy-start.16 = (f32[256]{0:T(256)S(1)}, f32[256]{0:T(256)}, u32[]{:S(2)}) copy-start(f32[256]{0:T(256)} %param.12) | copy-start | bytes 3076
  315.3 13.1 %copy-start.7 = (f32[1026,256]{1,0:T(8,128)S(1)}, f32[1026,256]{1,0:T(8,128)}, u32[]{:S(2)}) copy-start(f32[1026,256]{1,0:T(8,128)} %get-tuple-element.537) | copy-start | bytes 3151876
Sparse Core Ops, SparseCore 0:
  14.4 83.9 all-gather.6
  100.0 79.8 all-gather.8
  303.8 75.5 reduce-scatter.1
where the time goes:
time: 392 us; the launch traced here: 386 us
  waiting for transfers between devices  178 us (45%)
  matrix products  98.5 us (25%)
  other arithmetic  59.7 us (15%)
  local copies, waits for them, and re-layouts  22.8 us (6%)
  between operations  14.1 us (4%)
  blocking collectives  9.73 us (2%)
    dot_general x16, matrix products, matmul(): jnp.dot(left, right, preferred_element_type=jnp.float32, precision=lax.Pr...  98.5 us
    all_gather x1, waiting for transfers between devices, local(): lax.all_gather(own_grad_spec[None], 'ctx', axis=0, tiled=True)  81.4 us
    all_gather x1, waiting for transfers between devices, local(): lax.all_gather(own_gated_spec[None], 'ctx', axis=0, tiled=True)  50.6 us
    reduce_scatter x1, waiting for transfers between devices, local(): lax.psum_scatter(partial_value, 'ctx', scatter_dimension=0, tiled=True)  46.3 us
    mul x2, other arithmetic, inverse_table(): -weights * jnp.sin(angles)  22.1 us
    add x8, other arithmetic, conj_times(): real_a * real_b + imag_a * imag_b  12.8 us
    neg x2, other arithmetic, forward_table(): return jnp.concatenate([jnp.cos(angles), -jnp.sin(angles)], axis=0)  12.5 us
    psum x1, blocking collectives, local(): skip_grad = lax.psum(jnp.sum(mixed_grad * gated, axis=0), 'ctx')  9.73 us
  transfers between devices with their start and end apart: 3, of which 3 were waited for; matrix products, arithmetic and copies ran while one was open for 13% of the time, Pallas kernels for 0%

commit v1 on v0

--- a/solution.py
+++ b/solution.py
@@ -3,6 +3,27 @@
 import jax.numpy as jnp
 from jax import lax
 from jax.sharding import PartitionSpec as P
+
+
+def ring_gather(array, axis, dim):
+    size, position, span = (lax.axis_size(axis), lax.axis_index(axis), array.shape[dim])
+    forward = [(i, (i + 1) % size) for i in range(size)]
+    left = [(i, (i - 1) % size) for i in range(size)]
+    out = jnp.zeros((*array.shape[:dim], size * span, *array.shape[dim + 1 :]), array.dtype)
+    out = lax.dynamic_update_slice_in_dim(out, array, position * span, axis=dim)
+    from_left = from_right = array
+    half = size // 2
+    for step in range(1, half + 1):
+        from_left = lax.ppermute(from_left, axis, forward)
+        out = lax.dynamic_update_slice_in_dim(
+            out, from_left, (position - step) % size * span, axis=dim
+        )
+        if step < size - half:
+            from_right = lax.ppermute(from_right, axis, left)
+            out = lax.dynamic_update_slice_in_dim(
+                out, from_right, (position + step) % size * span, axis=dim
+            )
+    return out
 
 
 def matmul(left, right):
@@ -91,7 +112,7 @@
     )
     own_gated_spec = matmul(table_low, gated)
     pieces = (
-        lax.all_gather(own_gated_spec[None], "ctx", axis=0, tiled=True),
+        ring_gather(own_gated_spec[None], "ctx", 0),
         lax.all_gather(own_grad_spec[None], "ctx", axis=0, tiled=True),
     )
 

time: 392 us -> 378 us (0.964)
  waiting for transfers between devices: 178 us -> 105 us
  starting transfers between devices: 2.02 us -> 48.5 us
  local copies, waits for them, and re-layouts: 22.8 us -> 33.1 us
    all_gather x1, waiting for transfers between devices: 81.4 us -> 0.01 us  [local(): lax.all_gather(own_grad_spec[None], 'ctx', axis=0, tiled=True)]
    ppermute x0 -> x3, waiting for transfers between devices: none -> 58.7 us  [the longest x2 57.4 us: ring_gather(): from_left = lax.ppermute(from_left, axis, forward)]
    all_gather x1 -> x0, waiting for transfers between devices: 50.6 us -> none  [local(): lax.all_gather(own_gated_spec[None], 'ctx', axis=0, tiled=True)]
    ppermute x0 -> x3, starting transfers between devices: none -> 47.9 us  [the longest x2 45.6 us: ring_gather(): from_left = lax.ppermute(from_left, axis, forward)]
    broadcast_in_dim x0 -> x2, local copies, waits for them, and re-layouts: none -> 6.89 us  [the longest x1 4.58 us: local(): own_gated_spec[None]]
  transfers between devices with their start and end apart: 3 -> 5, of which waited for: 3 -> 4; matrix products, arithmetic and copies ran while one was open for 13% -> 17% of each run, Pallas kernels for 0% -> 0%
where the time goes in v1:
time: 378 us; the launch traced here: 372 us
  waiting for transfers between devices  105 us (28%)
  matrix products  98.6 us (26%)
  other arithmetic  63 us (17%)
  starting transfers between devices  48.5 us (13%)
  local copies, waits for them, and re-layouts  33.1 us (9%)
  between operations  14.5 us (4%)
  blocking collectives  9.58 us (3%)
    dot_general x16, matrix products, matmul(): jnp.dot(left, right, preferred_element_type=jnp.float32, precision=lax.Pr...  98.6 us
    ppermute x2, waiting for transfers between devices, ring_gather(): from_left = lax.ppermute(from_left, axis, forward)  57.4 us
    reduce_scatter x1, waiting for transfers between devices, local(): lax.psum_scatter(partial_value, 'ctx', scatter_dimension=0, tiled=True)  45.8 us
    ppermute x2, starting transfers between devices, ring_gather(): from_left = lax.ppermute(from_left, axis, forward)  45.6 us
    mul x2, other arithmetic, inverse_table(): -weights * jnp.sin(angles)  23.2 us
    neg x2, other arithmetic, forward_table(): return jnp.concatenate([jnp.cos(angles), -jnp.sin(angles)], axis=0)  12.5 us
    add x8, other arithmetic, conj_times(): real_a * real_b + imag_a * imag_b  12.3 us
    psum x1, blocking collectives, local(): skip_grad = lax.psum(jnp.sum(mixed_grad * gated, axis=0), 'ctx')  9.58 us
  transfers between devices with their start and end apart: 5, of which 4 were waited for; matrix products, arithmetic and copies ran while one was open for 17% of the time, Pallas kernels for 0%

profile of v1, /device:TPU:0, one launch (start us, length us, event | category | flops | bytes accessed | tf_op | source)
XLA Modules:
  0.0 372.2 jit_solution(119328479816475116)
XLA Ops:
  7.2 4.2 %fusion.71 = (f32[513,512]{1,0:T(8,128)S(1)}, f32[513,512]{1,0:T(8,128)S(1)}) fusion(s32[512]{0:T(512)S(1)} %iota_add_fusion), kind=kLoop, calls=%fused_computation.115 | loop fusion | flops 3939840 | bytes 2103296 | tf_op jit(solution)/shard_map/cos | solution.py:39
  11.5 2.8 fusion.32
  14.3 0.6 reduce-scatter.2.cloned.1.call-start
  14.9 4.2 %sine_negate_fusion.2 = (f32[513,512]{1,0:T(8,128)S(1)}, f32[513,512]{1,0:T(8,128)S(1)}) fusion(), kind=kLoop, calls=%fused_computation.105 | loop fusion | flops 3939840 | bytes 2101248 | tf_op jit(solution)/shard_map/neg | solution.py:39
  19.1 2.3 broadcast_in_dim.31
  21.4 2.8 constant_dynamic-update-slice_fusion.1
  24.2 4.6 %copy.12 = f32[1,1026,256]{2,0,1:T(1,128)S(1)} copy(f32[1,1026,256]{2,1,0:T(8,128)S(1)} %get-tuple-element.386) | data formatting | bytes 2101248 | tf_op jit(solution)/shard_map/broadcast_in_dim | solution.py:115
  28.8 3.1 collective-permute-start
  31.9 2.3 collective-permute-start.1
  34.2 8.4 %sine_negate_fusion = (f32[513,1024]{1,0:T(8,128)S(1)}, f32[513,1024]{1,0:T(8,128)S(1)}) fusion(), kind=kLoop, calls=%fused_computation.54 | loop fusion | flops 7879680 | bytes 4202496 | tf_op jit(solution)/shard_map/neg | solution.py:39
  42.5 2.7 pad_maximum_fusion.1
  45.2 11.6 %sine_multiply_fusion = (f32[1024,513]{1,0:T(8,128)}, f32[1024,513]{1,0:T(8,128)}) fusion(f32[513]{0:T(1024)S(1)} %fusion.73, f32[513]{0:T(1024)S(1)} %select_multiply_fusion), kind=kLoop, calls=%fused_computation.38 | loop fusion | flops 8404992 | bytes 4206600 | tf_op jit(solution)/shard_map/mul | solution.py:49
  56.8 5.5 %pad_maximum_fusion = f32[1024,1026]{1,0:T(8,128)} fusion(f32[1024,513]{1,0:T(8,128)} %get-tuple-element.394, f32[1024,513]{1,0:T(8,128)} %get-tuple-element.395), kind=kLoop, calls=%fused_computation.26 | loop fusion | flops 1050624 | bytes 8404992 | tf_op jit(solution)/shard_map/concatenate | solution.py:49
  62.3 18.2 %collective-permute-done = f32[1,1026,256]{2,0,1:T(1,128)S(1)} collective-permute-done((f32[1,1026,256]{2,0,1:T(1,128)S(1)}, f32[1,1026,256]{2,0,1:T(1,128)S(1)}, u32[]{:S(2)}, u32[]{:S(2)}) %collective-permute-start) | collective-permute-done | bytes 1050656 | tf_op jit(solution)/shard_map/ppermute | solution.py:17
  80.5 42.5 %collective-permute-start.2 = (f32[1,1026,256]{2,0,1:T(1,128)S(1)}, f32[1,1026,256]{2,0,1:T(1,128)S(1)}, u32[]{:S(2)}, u32[]{:S(2)}) collective-permute-start(f32[1,1026,256]{2,0,1:T(1,128)S(1)} %collective-permute-done), channel_id=1, source_target_pairs={{0,4},{4,8},{8,12},{12,0},{1,5},{5,9},{9,13},{13,1},{2,6},{6,10},{... | collective-permute-start | bytes 3151880 | tf_op jit(solution)/shard_map/ppermute | solution.py:17
  123.0 1.0 copy_dynamic-update-slice_fusion.2
  124.0 1.2 collective-permute-done.1
  125.3 1.1 copy_dynamic-update-slice_fusion.1
  126.3 39.2 %collective-permute-done.2 = f32[1,1026,256]{2,0,1:T(1,128)S(1)} collective-permute-done((f32[1,1026,256]{2,0,1:T(1,128)S(1)}, f32[1,1026,256]{2,0,1:T(1,128)S(1)}, u32[]{:S(2)}, u32[]{:S(2)}) %collective-permute-start.2) | collective-permute-done | bytes 1050656 | tf_op jit(solution)/shard_map/ppermute | solution.py:17
  165.6 1.1 copy_dynamic-update-slice_fusion
  166.6 2.3 broadcast_in_dim.30.clone
  168.9 120.8 %while.21 = (s32[]{:T(128)}, f32[1026,256]{1,0:T(8,128)}, f32[1026,256]{1,0:T(8,128)}, f32[4096,256]{1,0:T(8,128)}, s32[]{:T(128)}, /*index=5*/f32[4096,256]{1,0...) while((s32[]{:T(128)}, f32[1026,256]{1,0:T(8,128)}, ...), condition=%wide.region_1.2_spmd.clone, body=%wide.region_0.1_spmd.clone.sunk | while | flops 9687015424 | bytes 64113172 | solution.py:122
  168.9 5.7 %convolution_bitcast_fusion.6 = f32[1026,256]{1,0:T(8,128)S(1)} fusion(f32[1026,1024]{1,0:T(8,128)} %get-tuple-element.521, f32[4096,256]{1,0:T(8,128)} %get-tuple-element.520, s32[]{:T(128)S(6)} %select_n.200), kind=kOutput, calls=%fused_computation.1.clone.1 | convolution fusion | flops 3227516928 | bytes 6326276 | tf_op jit(solution)/shard_map/while/body/eval_jaxpr/dot_general | solution.py:30
  174.6 1.5 multiply_add_fusion.5
  176.1 5.7 %convolution_bitcast_fusion.7 = f32[1026,256]{1,0:T(8,128)S(1)} fusion(f32[1026,1024]{1,0:T(8,128)} %get-tuple-element.521, f32[4096,256]{1,0:T(8,128)} %get-tuple-element.520, s32[]{:T(128)S(6)} %select_n.201), kind=kOutput, calls=%fused_computation.clone.1 | convolution fusion | flops 3227516928 | bytes 6326276 | tf_op jit(solution)/shard_map/while/body/eval_jaxpr/dot_general | solution.py:30
  181.9 1.5 multiply_add_fusion.6
  183.7 0.6 maximum_add_fusion.3
  184.4 1.0 copy-done.3
  185.7 1.3 constant_dynamic-slice_fusion.2
  187.3 9.8 %fusion.98 = f32[1024,256]{0,1:T(8,128)S(1)} fusion(f32[1024,256]{0,1:T(8,128)S(1)} %copy.27, f32[1024,1026]{1,0:T(8,128)} %get-tuple-element.525, f32[513,256]{1,0:T(8,128)S(1)} %get-tuple-element.477, f32[513,256]{1,0:T(8,128)S(1)} %get-tuple-element.478), kind=kOutput, calls=%fused_computation.3.clone.1 | convolution fusion | flops 3228041728 | bytes 7350272 | tf_op jit(solution)/shard_map/while/body/eval_jaxpr/dot_general | solution.py:30
  197.5 1.1 constant_dynamic-update-slice_fusion.3
  199.1 5.7 %convolution_bitcast_fusion.6 = f32[1026,256]{1,0:T(8,128)S(1)} fusion(f32[1026,1024]{1,0:T(8,128)} %get-tuple-element.521, f32[4096,256]{1,0:T(8,128)} %get-tuple-element.520, s32[]{:T(128)S(6)} %select_n.200), kind=kOutput, calls=%fused_computation.1.clone.1 | convolution fusion | flops 3227516928 | bytes 6326276 | tf_op jit(solution)/shard_map/while/body/eval_jaxpr/dot_general | solution.py:30
  204.8 1.5 multiply_add_fusion.5
  206.3 5.7 %convolution_bitcast_fusion.7 = f32[1026,256]{1,0:T(8,128)S(1)} fusion(f32[1026,1024]{1,0:T(8,128)} %get-tuple-element.521, f32[4096,256]{1,0:T(8,128)} %get-tuple-element.520, s32[]{:T(128)S(6)} %select_n.201), kind=kOutput, calls=%fused_computation.clone.1 | convolution fusion | flops 3227516928 | bytes 6326276 | tf_op jit(solution)/shard_map/while/body/eval_jaxpr/dot_general | solution.py:30
  212.1 1.5 multiply_add_fusion.6
  213.9 0.6 maximum_add_fusion.3
  214.6 1.0 copy-done.3
  215.9 1.3 constant_dynamic-slice_fusion.2
  217.5 9.8 %fusion.98 = f32[1024,256]{0,1:T(8,128)S(1)} fusion(f32[1024,256]{0,1:T(8,128)S(1)} %copy.27, f32[1024,1026]{1,0:T(8,128)} %get-tuple-element.525, f32[513,256]{1,0:T(8,128)S(1)} %get-tuple-element.477, f32[513,256]{1,0:T(8,128)S(1)} %get-tuple-element.478), kind=kOutput, calls=%fused_computation.3.clone.1 | convolution fusion | flops 3228041728 | bytes 7350272 | tf_op jit(solution)/shard_map/while/body/eval_jaxpr/dot_general | solution.py:30
  227.7 1.1 constant_dynamic-update-slice_fusion.3
  229.3 5.7 %convolution_bitcast_fusion.6 = f32[1026,256]{1,0:T(8,128)S(1)} fusion(f32[1026,1024]{1,0:T(8,128)} %get-tuple-element.521, f32[4096,256]{1,0:T(8,128)} %get-tuple-element.520, s32[]{:T(128)S(6)} %select_n.200), kind=kOutput, calls=%fused_computation.1.clone.1 | convolution fusion | flops 3227516928 | bytes 6326276 | tf_op jit(solution)/shard_map/while/body/eval_jaxpr/dot_general | solution.py:30
  235.0 1.5 multiply_add_fusion.5
  236.5 5.7 %convolution_bitcast_fusion.7 = f32[1026,256]{1,0:T(8,128)S(1)} fusion(f32[1026,1024]{1,0:T(8,128)} %get-tuple-element.521, f32[4096,256]{1,0:T(8,128)} %get-tuple-element.520, s32[]{:T(128)S(6)} %select_n.201), kind=kOutput, calls=%fused_computation.clone.1 | convolution fusion | flops 3227516928 | bytes 6326276 | tf_op jit(solution)/shard_map/while/body/eval_jaxpr/dot_general | solution.py:30
  242.3 1.5 multiply_add_fusion.6
  244.1 0.6 maximum_add_fusion.3
  244.8 1.0 copy-done.3
  246.1 1.3 constant_dynamic-slice_fusion.2
  247.7 9.8 %fusion.98 = f32[1024,256]{0,1:T(8,128)S(1)} fusion(f32[1024,256]{0,1:T(8,128)S(1)} %copy.27, f32[1024,1026]{1,0:T(8,128)} %get-tuple-element.525, f32[513,256]{1,0:T(8,128)S(1)} %get-tuple-element.477, f32[513,256]{1,0:T(8,128)S(1)} %get-tuple-element.478), kind=kOutput, calls=%fused_computation.3.clone.1 | convolution fusion | flops 3228041728 | bytes 7350272 | tf_op jit(solution)/shard_map/while/body/eval_jaxpr/dot_general | solution.py:30
  257.9 1.0 constant_dynamic-update-slice_fusion.3
  258.9 0.6 copy-done.1
  259.5 5.7 %convolution_bitcast_fusion.6 = f32[1026,256]{1,0:T(8,128)S(1)} fusion(f32[1026,1024]{1,0:T(8,128)} %get-tuple-element.521, f32[4096,256]{1,0:T(8,128)} %get-tuple-element.520, s32[]{:T(128)S(6)} %select_n.200), kind=kOutput, calls=%fused_computation.1.clone.1 | convolution fusion | flops 3227516928 | bytes 6326276 | tf_op jit(solution)/shard_map/while/body/eval_jaxpr/dot_general | solution.py:30
  265.2 1.5 multiply_add_fusion.5
  266.7 5.7 %convolution_bitcast_fusion.7 = f32[1026,256]{1,0:T(8,128)S(1)} fusion(f32[1026,1024]{1,0:T(8,128)} %get-tuple-element.521, f32[4096,256]{1,0:T(8,128)} %get-tuple-element.520, s32[]{:T(128)S(6)} %select_n.201), kind=kOutput, calls=%fused_computation.clone.1 | convolution fusion | flops 3227516928 | bytes 6326276 | tf_op jit(solution)/shard_map/while/body/eval_jaxpr/dot_general | solution.py:30
  272.5 1.5 multiply_add_fusion.6
  274.3 0.6 maximum_add_fusion.3
  275.0 1.0 copy-done.3
  276.3 1.3 constant_dynamic-slice_fusion.2
  277.9 9.8 %fusion.98 = f32[1024,256]{0,1:T(8,128)S(1)} fusion(f32[1024,256]{0,1:T(8,128)S(1)} %copy.27, f32[1024,1026]{1,0:T(8,128)} %get-tuple-element.525, f32[513,256]{1,0:T(8,128)S(1)} %get-tuple-element.477, f32[513,256]{1,0:T(8,128)S(1)} %get-tuple-element.478), kind=kOutput, calls=%fused_computation.3.clone.1 | convolution fusion | flops 3228041728 | bytes 7350272 | tf_op jit(solution)/shard_map/while/body/eval_jaxpr/dot_general | solution.py:30
  288.1 1.1 constant_dynamic-update-slice_fusion.3
  289.8 11.6 %sine_multiply_fusion.1 = (f32[512,513]{1,0:T(8,128)S(1)}, f32[512,513]{1,0:T(8,128)S(1)}, f32[512,513]{1,0:T(8,128)}, f32[512,513]{1,0:T(8,128)S(1)}) fusion(f32[513]{0:T(1024)S(1)} %fusion.73, s32[512]{0:T(512)S(1)} %iota_add_fusion, f32[513]{0:T(1024)S(1)} %select_multiply_fusion), kind=kLoop, calls=%fused_computation.83 | loop fusion | flops 8404992 | bytes 4208648 | tf_op jit(solution)/shard_map/mul | solution.py:49
  301.5 3.3 multiply_reduce_fusion
  304.8 9.6 %psum.7 = f32[256]{0:T(256)} all-reduce(f32[256]{0:T(256)S(1)} %get-tuple-element.376), channel_id=1, replica_groups=mesh['groups'=2,'ctx'=4,'chan'=4] {'ctx'}, use_global_device_ids=true, to_apply=%region_4.5 | all-reduce | flops 256 | bytes 2048 | tf_op jit(solution)/shard_map/psum | solution.py:130
  314.4 4.9 %fusion.54 = f32[512,256]{1,0:T(8,128)} fusion(f32[512,256]{1,0:T(8,128)} %param.13, f32[1026,256]{1,0:T(8,128)S(1)} %copy-done.7, f32[512,513]{1,0:T(8,128)S(1)} %get-tuple-element.382, f32[512,513]{1,0:T(8,128)} %get-tuple-element.392, f32[256]{0:T(256)S(1)} %copy-done.16, f32[512,256]{1,0:T(8,128)} %param.9, f32[512,256]{1,0:T(8,128)} %param.10), kind=kOutput, calls=%fused_computation.95 | convolution fusion | flops 1614808064 | bytes 5250048 | tf_op jit(solution)/shard_map/dot_general | solution.py:30
  319.2 45.8 %reduce-scatter.2.cloned.1.call-done = f32[1024,256]{1,0:T(8,128)} async-done(((f32[4096,256]{1,0:T(8,128)}), f32[1024,256]{1,0:T(8,128)}) %reduce-scatter.2.cloned.1.call-update) | async-done | bytes 1048592 | tf_op jit(solution)/shard_map/reduce_scatter | solution.py:124
  (76 shorter events, 6.7 us)
Async XLA Ops:
  7.2 4.3 %copy-start.8 = (f32[512,256]{1,0:T(8,128)S(1)}, f32[512,256]{1,0:T(8,128)}, u32[]{:S(2)}) copy-start(f32[512,256]{1,0:T(8,128)} %param.13) | copy-start | bytes 1572868
  7.2 4.3 %copy-start.14 = (f32[512,256]{1,0:T(8,128)S(1)}, f32[512,256]{1,0:T(8,128)}, u32[]{:S(2)}) copy-start(f32[512,256]{1,0:T(8,128)} %param.8) | copy-start | bytes 1572868
  7.2 159.5 %all-gather.4.cloned.1.call-start = ((), (), s32[]{:S(2)}) async-start(), calls=%async_computation.2 | async-start | bytes 5283840 | tf_op jit(solution)/shard_map/all_gather | solution.py:116
  14.3 350.7 %reduce-scatter.2.cloned.1.call-start = ((), (), s32[]{:S(2)}) async-start(), calls=%async_computation.1 | async-start | bytes 5242880 | tf_op jit(solution)/shard_map/reduce_scatter | solution.py:124
  19.1 2.3 copy-start.10
  19.1 2.3 copy-start.12
  28.8 51.6 %collective-permute-start = (f32[1,1026,256]{2,0,1:T(1,128)S(1)}, f32[1,1026,256]{2,0,1:T(1,128)S(1)}, u32[]{:S(2)}, u32[]{:S(2)}) collective-permute-start(f32[1,1026,256]{2,0,1:T(1,128)S(1)} %copy.12), channel_id=1, source_target_pairs={{0,4},{4,8},{8,12},{12,0},{1,5},{5,9},{9,13},{13,1},{2,6},{6,10},{... | collective-permute-start | bytes 3151880 | tf_op jit(solution)/shard_map/ppermute | solution.py:17
  31.9 93.4 %collective-permute-start.1 = (f32[1,1026,256]{2,0,1:T(1,128)S(1)}, f32[1,1026,256]{2,0,1:T(1,128)S(1)}, u32[]{:S(2)}, u32[]{:S(2)}) collective-permute-start(f32[1,1026,256]{2,0,1:T(1,128)S(1)} %copy.12), channel_id=1, source_target_pairs={{0,12},{4,0},{8,4},{12,8},{1,13},{5,1},{9,5},{13,9},{2,14},{6,2},{... | collective-permute-start | bytes 3151880 | tf_op jit(solution)/shard_map/ppermute | solution.py:22
  80.5 85.1 %collective-permute-start.2 = (f32[1,1026,256]{2,0,1:T(1,128)S(1)}, f32[1,1026,256]{2,0,1:T(1,128)S(1)}, u32[]{:S(2)}, u32[]{:S(2)}) collective-permute-start(f32[1,1026,256]{2,0,1:T(1,128)S(1)} %collective-permute-done), channel_id=1, source_target_pairs={{0,4},{4,8},{8,12},{12,0},{1,5},{5,9},{9,13},{13,1},{2,6},{6,10},{... | collective-permute-start | bytes 3151880 | tf_op jit(solution)/shard_map/ppermute | solution.py:17
  166.6 2.3 copy-start
  181.8 1.6 copy-start.2
  181.9 1.9 copy-start.5
  184.3 1.0 copy-start.3
  184.4 1.3 copy-start.6
  197.5 1.6 copy-start.1
  212.0 1.6 copy-start.2
  212.0 1.9 copy-start.5
  214.5 1.0 copy-start.3
  214.6 1.3 copy-start.6
  227.7 1.6 copy-start.1
  242.2 1.6 copy-start.2
  242.2 1.9 copy-start.5
  244.7 1.0 copy-start.3
  244.7 1.3 copy-start.6
  257.9 1.6 copy-start.1
  272.4 1.6 copy-start.2
  272.4 1.9 copy-start.5
  274.9 1.0 copy-start.3
  274.9 1.3 copy-start.6
  288.1 1.6 copy-start.1
  289.7 11.7 %copy-start.4 = (f32[1026,256]{1,0:T(8,128)S(1)}, f32[1026,256]{1,0:T(8,128)}, u32[]{:S(2)}) copy-start(f32[1026,256]{1,0:T(8,128)} %get-tuple-element.539) | copy-start | bytes 3151876
  289.7 11.7 %copy-start.9 = (f32[512,256]{1,0:T(8,128)S(1)}, f32[512,256]{1,0:T(8,128)}, u32[]{:S(2)}) copy-start(f32[512,256]{1,0:T(8,128)} %param.13) | copy-start | bytes 1572868
  289.7 11.7 %copy-start.11 = (f32[512,256]{1,0:T(8,128)S(1)}, f32[512,256]{1,0:T(8,128)}, u32[]{:S(2)}) copy-start(f32[512,256]{1,0:T(8,128)} %param.9) | copy-start | bytes 1572868
  289.8 11.7 %copy-start.13 = (f32[512,256]{1,0:T(8,128)S(1)}, f32[512,256]{1,0:T(8,128)}, u32[]{:S(2)}) copy-start(f32[512,256]{1,0:T(8,128)} %param.10) | copy-start | bytes 1572868
  289.8 11.7 %copy-start.15 = (f32[512,256]{1,0:T(8,128)S(1)}, f32[512,256]{1,0:T(8,128)}, u32[]{:S(2)}) copy-start(f32[512,256]{1,0:T(8,128)} %param.8) | copy-start | bytes 1572868
  289.8 11.7 %copy-start.16 = (f32[256]{0:T(256)S(1)}, f32[256]{0:T(256)}, u32[]{:S(2)}) copy-start(f32[256]{0:T(256)} %param.12) | copy-start | bytes 3076
  301.5 12.9 %copy-start.7 = (f32[1026,256]{1,0:T(8,128)S(1)}, f32[1026,256]{1,0:T(8,128)}, u32[]{:S(2)}) copy-start(f32[1026,256]{1,0:T(8,128)} %get-tuple-element.538) | copy-start | bytes 3151876
Sparse Core Ops, SparseCore 0:
  14.4 143.8 all-gather.3
  289.8 75.1 reduce-scatter.1
